TPU v7x, 256 devices: a whole 4x4x8 slice. The times are simulated.
256 devices in a mesh: gx: 32 (over x_hi, z, core), gy: 8 (over x_lo, y).
Axes of the slice: x: 4 (x_hi: 2, x_lo: 2; x = x_hi * 2 + x_lo), y: 4, z: 8, core: 2. Of those that a mesh axis runs over, the one named last changes fastest.
Arguments:
- chemical_share_array: float32 [16, 8, 1024, 2048], P(None, None, 'gx', 'gy'), may hold values from 0 to 1
- horizontal_motion: float32 [8, 1024, 2048], P(None, 'gx', 'gy'), may hold values from -8 to 8
- vertical_motion: float32 [8, 1024, 2048], P(None, 'gx', 'gy'), may hold values from -8 to 8
- nondimensional_thermal_value: float32 [8, 1024, 2048], P(None, 'gx', 'gy'), may hold values from 0.8 to 2
- collision_prefactors_array: float32 [32], replicated, may hold values from 0.3 to 3
- activation_thresholds: float32 [32], replicated, may hold values from 0.5 to 4
- stoichiometry_table: float32 [32, 16], replicated, may hold values from -4 to 4
- transverse_loading_horizontal: float32 [1024, 64], P('gx'), may hold values from -0.1875 to 0.1875
- transverse_loading_vertical: float32 [2048, 64], P('gy'), may hold values from -0.125 to 0.125
Outputs:
- new_state: float32 [16, 8, 1024, 2048], P(None, None, 'gx', 'gy')
- core_part: float32 [64, 64, 128], P('gx', 'gy')
All inputs are finite; a program needn't handle non-finite values.
Results may differ from a plain program's by a relative error of at most 0.000094.
Values sent between devices are 32-bit elements; how exact they have to be, the bound alone decides.
A program may use at most 128 MiB of HBM per device.

v0:
```python
import jax
import jax.numpy as jnp
import numpy as np
from jax import lax
from jax.sharding import PartitionSpec as P

NS = 16
RATE_LAWS_TOTAL = 32


first_coef = (0.8, -0.2, 4.0 / 105.0, -1.0 / 280.0)
second_coef = (-205.0 / 72.0, 1.6, -0.2, 8.0 / 315.0, -1.0 / 560.0)
step_size = 0.5
diffusivity = 0.2


def with_halo(shard, sides, width):
    for axis, dim in sides:
        size, length = (lax.axis_size(axis), shard.shape[dim])
        up = [(i, (i + 1) % size) for i in range(size)]
        down = [(j, i) for i, j in up]
        last = lax.slice_in_dim(shard, length - width, length, axis=dim)
        leading = lax.slice_in_dim(shard, 0, width, axis=dim)
        before = lax.ppermute(last, axis, up)
        after = lax.ppermute(leading, axis, down)
        shard = jnp.concatenate([before, shard, after], axis=dim)
    return shard


def stencil_terms(padded, axis, length):
    center = lax.slice_in_dim(padded, 4, 4 + length, axis=axis)
    first_sum = jnp.zeros_like(center)
    second_sum = second_coef[0] * center
    for offset in range(1, 5):
        ahead = lax.slice_in_dim(padded, 4 + offset, 4 + offset + length, axis=axis)
        behind = lax.slice_in_dim(padded, 4 - offset, 4 - offset + length, axis=axis)
        first_sum = first_sum + first_coef[offset - 1] * (ahead - behind)
        second_sum = second_sum + second_coef[offset] * (ahead + behind)
    return (first_sum, second_sum)


def shards(
    chemical_share_array,
    horizontal_motion,
    vertical_motion,
    nondimensional_thermal_value,
    collision_prefactors_array,
    activation_thresholds,
    stoichiometry_table,
    transverse_loading_horizontal,
    transverse_loading_vertical,
):
    cells_x = chemical_share_array.shape[2]
    cells_y = chemical_share_array.shape[3]
    species = chemical_share_array.shape[0]
    pile_of_pages = chemical_share_array.shape[1]
    padded = with_halo(chemical_share_array, (("gx", 2), ("gy", 3)), 4)
    along_x = padded[:, :, :, 4 : 4 + cells_y]
    along_y = padded[:, :, 4 : 4 + cells_x, :]
    slope_x, curve_x = stencil_terms(along_x, 2, cells_x)
    slope_y, curve_y = stencil_terms(along_y, 3, cells_y)
    first_idx = np.arange(RATE_LAWS_TOTAL) % NS
    second_idx = (3 * np.arange(RATE_LAWS_TOTAL) + 1) % NS
    thermal_rate_law = collision_prefactors_array[:, None, None, None] * jnp.exp(
        -activation_thresholds[:, None, None, None] / nondimensional_thermal_value[None]
    )
    products = thermal_rate_law * chemical_share_array[first_idx] * chemical_share_array[second_idx]
    source = jnp.einsum(
        "rs,rzxy->szxy", stoichiometry_table, products, precision=lax.Precision.HIGHEST
    )
    rhs = -horizontal_motion[None] * slope_x - vertical_motion[None] * slope_y
    rhs = rhs + diffusivity * (curve_x + curve_y) + source
    new_state = chemical_share_array + step_size * rhs
    partial_y = jnp.einsum(
        "szxy,yj->szxj", new_state, transverse_loading_vertical, precision=lax.Precision.HIGHEST
    )
    rank_size = transverse_loading_horizontal.shape[1]
    partial_core = jnp.einsum(
        "xi,szxj->ijsz", transverse_loading_horizontal, partial_y, precision=lax.Precision.HIGHEST
    )
    partial_core = partial_core.reshape(rank_size, rank_size, species * pile_of_pages)
    reduced = lax.psum_scatter(partial_core, "gy", scatter_dimension=1, tiled=True)
    core_part = lax.psum_scatter(reduced, "gx", scatter_dimension=0, tiled=True)
    return (new_state, core_part)


def solution(mesh):
    in_specs = (
        P(None, None, "gx", "gy"),
        P(None, "gx", "gy"),
        P(None, "gx", "gy"),
        P(None, "gx", "gy"),
        P(),
        P(),
        P(),
        P("gx", None),
        P("gy", None),
    )
    out_specs = (P(None, None, "gx", "gy"), P("gx", "gy", None))
    return jax.shard_map(shards, mesh=mesh, in_specs=in_specs, out_specs=out_specs, check_vma=False)
```

profile of v0, /device:TPU:1, one launch (start us, length us, event | category | flops | bytes accessed | tf_op | source)
XLA Modules:
  0.0 290.2 jit_solution(10480677836372451162)
XLA Ops:
  7.2 0.0 copy-start
  7.2 0.0 copy-start.9
  7.2 0.0 copy-start.10
  7.2 0.0 copy-start.12
  7.2 0.0 reduce-scatter.3.cloned.1.call-start
  7.3 1.8 fusion.21
  9.0 0.3 copy.50
  9.3 3.1 %collective-permute-start.1 = (f32[16,8,4,256]{3,0,2,1:T(8,128)S(1)}, f32[16,8,4,256]{3,0,2,1:T(8,128)S(1)}, u32[]{:S(2)}, u32[]{:S(2)}) collective-permute-start(f32[16,8,4,256]{3,0,2,1:T(8,128)S(1)} %copy.50), channel_id=1, source_target_pairs={{0,8},{8,16},{16,24},{24,32},{32,40},{40,48},{48,56},{56,64},{64,7... | collective-permute-start | bytes 1572872 | tf_op jit(solution)/shard_map/ppermute | solution.py:24
  12.4 0.3 copy.51
  12.7 0.3 collective-permute-start
  13.0 0.0 copy-done.12
  13.0 0.0 copy-done.9
  13.0 0.0 copy-done.10
  13.1 6.5 %gather_fusion.1 = f32[32,8,32,256]{3,2,1,0:T(8,128)} fusion(f32[16,8,32,256]{3,2,1,0:T(8,128)} %param.13, s32[1024]{0:T(1024)S(1)} %get-tuple-element.17), kind=kCustom, calls=%fused_computation.1 | custom fusion | bytes 16777344 | tf_op jit(solution)/shard_map/gather | solution.py:67
  19.5 6.5 %gather_fusion = f32[32,8,32,256]{3,2,1,0:T(8,128)} fusion(f32[16,8,32,256]{3,2,1,0:T(8,128)} %param.13, s32[1024]{0:T(1024)S(1)} %get-tuple-element.18), kind=kCustom, calls=%fused_computation | custom fusion | bytes 16777344 | tf_op jit(solution)/shard_map/gather | solution.py:67
  26.1 0.0 collective-permute-done.1
  26.1 0.1 constant_dynamic-update-slice_fusion.3
  26.2 5.6 %constant_dynamic-update-slice_fusion.1 = (f32[16,8,36,256]{3,0,2,1:T(8,128)S(1)}, f32[16,8,36,256]{3,0,2,1:T(8,128)S(1)}, f32[16,8,40,256]{3,0,2,1:T(8,128)S(1)}) fusion(f32[16,8,32,256]{3,2,1,0:T(8,128)} %param.13, f32[16,8,36,256]{3,0,2,1:T(8,128)S(1)} %get-tuple-element.15, f32[16,8,40,256]{3,0,2,1:T(8,128)S(1)} %get-tuple-element.16), kind=kLoop, calls=%fused_computation.36 | loop fusion | bytes 16777216
  31.8 0.0 copy-start.6
  31.8 0.0 collective-permute-done
  31.8 0.1 constant_dynamic-update-slice_fusion
  32.0 0.0 copy-start.2
  32.0 0.0 copy-start.3
  32.0 2.0 copy-done.6
  34.0 3.0 %fusion.20 = (f32[16,8,40,4]{3,0,2,1:T(8,128)}, f32[16,8,40,4]{3,0,2,1:T(8,128)S(1)}) fusion(f32[16,8,40,256]{3,0,2,1:T(8,128)S(1)} %get-tuple-element.14), kind=kLoop, calls=%fused_computation.45 | loop fusion | bytes 327680 | tf_op jit(solution)/shard_map/slice | solution.py:22
  37.0 0.0 copy-done.2
  37.1 0.8 copy-done.3
  37.8 0.0 copy-start.4
  37.8 0.0 copy-start.8
  37.8 3.8 %copy.32 = f32[16,8,40,4]{2,1,3,0:T(8,128)} copy(f32[16,8,40,4]{3,0,2,1:T(8,128)} %get-tuple-element.6) | data formatting | bytes 163840 | tf_op jit(solution)/shard_map/slice | solution.py:22
  41.6 1.4 copy.30
  43.0 0.0 copy-start.5
  43.0 3.6 %collective-permute-start.2 = (f32[16,8,40,4]{2,1,3,0:T(8,128)S(1)}, f32[16,8,40,4]{2,1,3,0:T(8,128)S(1)}, u32[]{:S(2)}, u32[]{:S(2)}) collective-permute-start(f32[16,8,40,4]{2,1,3,0:T(8,128)S(1)} %copy.30), channel_id=1, source_target_pairs={{1,0},{2,1},{3,2},{4,3},{5,4},{6,5},{7,6},{0,7},{9,8},{10,9},{11,1... | collective-permute-start | bytes 245768 | tf_op jit(solution)/shard_map/ppermute | solution.py:25
  46.6 0.0 collective-permute-start.3
  46.6 0.0 copy-done.4
  46.6 0.0 copy-done.8
  46.6 9.5 %fusion.2 = f32[32,8,32,256]{3,2,1,0:T(8,128)} fusion(f32[32,8,32,256]{3,2,1,0:T(8,128)} %gather_fusion.1, f32[32,8,32,256]{3,2,1,0:T(8,128)} %gather_fusion, f32[8,32,256]{2,1,0:T(8,128)S(1)} %copy-done.4, f32[32]{0:T(128)S(1)} %neg.9, f32[32]{0:T(128)S(1)} %copy-done.8), kind=kLoop, calls=%fused_computation.17 | loop fusion | flops 8388608 | bytes 25428224 | tf_op jit(solution)/shard_map/mul | solution.py:67
  56.1 0.0 copy-done.5
  56.1 0.0 copy-start.11
  56.1 0.0 collective-permute-done.3
  56.1 2.1 copy.33
  58.2 0.0 collective-permute-done.2
  58.2 2.5 copy.31
  60.8 0.0 copy-done.11
  60.8 38.4 %fusion.12 = f32[16,8,32,256]{3,0,2,1:T(8,128)} fusion(f32[16,8,40,4]{3,0,2,1:T(8,128)} %copy.31, f32[16,8,40,256]{3,0,2,1:T(8,128)} %copy-done.2, f32[16,8,40,4]{3,0,2,1:T(8,128)S(1)} %copy.33, f32[16,8,36,256]{3,0,2,1:T(8,128)} %copy-done.6, f32[16,8,36,256]{3,0,2,1:T(8,128)} %copy-done.3, f32[32,8,32,256]{3,2,1,0:T(8,128)} %fusion.2, ...), kind=kOutput, calls=%fused_computation.30 | convolution fusion | flops 469762048 | bytes 56264704 | tf_op jit(solution)/shard_map/rs,rzxy->szxy/dot_general | solution.py:68
  99.2 4.6 %copy.38 = f32[16,8,32,256]{3,2,1,0:T(8,128)S(1)} copy(f32[16,8,32,256]{3,0,2,1:T(8,128)} %fusion.12) | data formatting | bytes 8388608
  103.8 0.0 copy-done
  103.8 0.0 copy-start.1
  103.8 0.0 copy-start.7
  103.8 3.6 %fusion.15 = f32[16,8,32,64]{3,2,1,0:T(8,128)S(1)} fusion(f32[16,8,32,256]{3,2,1,0:T(8,128)S(1)} %copy.38, f32[256,64]{0,1:T(8,128)S(1)} %copy-done), kind=kOutput, calls=%fused_computation.31 | convolution fusion | flops 805306368 | bytes 5308416 | tf_op jit(solution)/shard_map/szxy,yj->szxj/dot_general | solution.py:74
  107.5 0.0 copy-done.7
  107.5 8.3 %fusion.17 = f32[16,8,64,64]{3,2,1,0:T(8,128)} fusion(f32[16,8,32,64]{3,2,1,0:T(8,128)S(1)} %fusion.15, f32[32,64]{1,0:T(8,128)S(1)} %copy-done.7), kind=kOutput, calls=%fused_computation.33 | convolution fusion | flops 201326592 | bytes 3153920 | tf_op jit(solution)/shard_map/xi,szxj->ijsz/dot_general | solution.py:78
  115.8 0.0 copy-done.1
  115.8 5.3 %copy.37 = f32[64,64,128]{2,1,0:T(8,128)} copy(f32[64,64,128]{0,1,2:T(8,128)} %bitcast.26) | data formatting | bytes 4194304 | tf_op jit(solution)/shard_map/reshape | solution.py:81
  121.1 0.0 reduce-scatter.3.cloned.1.call-update
  121.1 0.0 reduce-scatter.5.cloned.1.call-start
  121.1 44.4 %reduce-scatter.3.cloned.1.call-done = f32[64,8,128]{2,1,0:T(8,128)} async-done(((f32[64,64,128]{2,1,0:T(8,128)}), f32[64,8,128]{2,1,0:T(8,128)}) %reduce-scatter.3.cloned.1.call-update) | async-done | bytes 262160 | tf_op jit(solution)/shard_map/reduce_scatter | solution.py:82
  165.5 0.0 reduce-scatter.5.cloned.1.call-update
  165.6 117.8 %reduce-scatter.5.cloned.1.call-done = f32[2,8,128]{2,1,0:T(8,128)} async-done(((f32[64,8,128]{2,1,0:T(8,128)}), f32[2,8,128]{2,1,0:T(8,128)}) %reduce-scatter.5.cloned.1.call-update) | async-done | bytes 8208 | tf_op jit(solution)/shard_map/reduce_scatter | solution.py:83
  (3 shorter events, 0.0 us)
Async XLA Ops:
  7.2 96.6 %copy-start = (f32[256,64]{0,1:T(8,128)S(1)}, f32[256,64]{0,1:T(8,128)}, u32[]{:S(2)}) copy-start(f32[256,64]{0,1:T(8,128)} %param.21) | copy-start | bytes 196612
  7.2 5.9 %copy-start.9 = (s32[32]{0:T(128)S(1)}, s32[32]{0:T(128)}, u32[]{:S(2)}) copy-start(s32[32]{0:T(128)} %constant.34) | copy-start | bytes 388
  7.2 5.8 %copy-start.10 = (s32[32]{0:T(128)S(1)}, s32[32]{0:T(128)}, u32[]{:S(2)}) copy-start(s32[32]{0:T(128)} %constant.33) | copy-start | bytes 388
  7.2 5.8 %copy-start.12 = (f32[32]{0:T(128)S(1)}, f32[32]{0:T(128)}, u32[]{:S(2)}) copy-start(f32[32]{0:T(128)} %param.18) | copy-start | bytes 388
  7.2 158.3 %reduce-scatter.3.cloned.1.call-start = ((), (), s32[]{:S(2)}) async-start(), calls=%async_computation.2 | async-start | bytes 2359296 | tf_op jit(solution)/shard_map/reduce_scatter | solution.py:82
  9.3 16.7 %collective-permute-start.1 = (f32[16,8,4,256]{3,0,2,1:T(8,128)S(1)}, f32[16,8,4,256]{3,0,2,1:T(8,128)S(1)}, u32[]{:S(2)}, u32[]{:S(2)}) collective-permute-start(f32[16,8,4,256]{3,0,2,1:T(8,128)S(1)} %copy.50), channel_id=1, source_target_pairs={{0,8},{8,16},{16,24},{24,32},{32,40},{40,48},{48,56},{56,64},{64,7... | collective-permute-start | bytes 1572872 | tf_op jit(solution)/shard_map/ppermute | solution.py:24
  12.7 19.1 %collective-permute-start = (f32[16,8,4,256]{3,0,2,1:T(8,128)S(1)}, f32[16,8,4,256]{3,0,2,1:T(8,128)S(1)}, u32[]{:S(2)}, u32[]{:S(2)}) collective-permute-start(f32[16,8,4,256]{3,0,2,1:T(8,128)S(1)} %copy.51), channel_id=1, source_target_pairs={{8,0},{16,8},{24,16},{32,24},{40,32},{48,40},{56,48},{64,56},{72,6... | collective-permute-start | bytes 1572872 | tf_op jit(solution)/shard_map/ppermute | solution.py:25
  31.8 2.2 copy-start.6
  32.0 5.1 %copy-start.2 = (f32[16,8,40,256]{3,0,2,1:T(8,128)}, f32[16,8,40,256]{3,0,2,1:T(8,128)S(1)}, u32[]{:S(2)}) copy-start(f32[16,8,40,256]{3,0,2,1:T(8,128)S(1)} %get-tuple-element.14) | copy-start | bytes 15728644
  32.0 5.8 %copy-start.3 = (f32[16,8,36,256]{3,0,2,1:T(8,128)}, f32[16,8,36,256]{3,0,2,1:T(8,128)S(1)}, u32[]{:S(2)}) copy-start(f32[16,8,36,256]{3,0,2,1:T(8,128)S(1)} %get-tuple-element.13) | copy-start | bytes 14155780
  37.8 8.8 %copy-start.4 = (f32[8,32,256]{2,1,0:T(8,128)S(1)}, f32[8,32,256]{2,1,0:T(8,128)}, u32[]{:S(2)}) copy-start(f32[8,32,256]{2,1,0:T(8,128)} %param.16) | copy-start | bytes 786436
  37.8 8.8 %copy-start.8 = (f32[32]{0:T(128)S(1)}, f32[32]{0:T(128)}, u32[]{:S(2)}) copy-start(f32[32]{0:T(128)} %param.17) | copy-start | bytes 388
  43.0 13.0 %copy-start.5 = (f32[8,32,256]{2,1,0:T(8,128)S(1)}, f32[8,32,256]{2,1,0:T(8,128)}, u32[]{:S(2)}) copy-start(f32[8,32,256]{2,1,0:T(8,128)} %param.14) | copy-start | bytes 786436
  43.0 15.2 %collective-permute-start.2 = (f32[16,8,40,4]{2,1,3,0:T(8,128)S(1)}, f32[16,8,40,4]{2,1,3,0:T(8,128)S(1)}, u32[]{:S(2)}, u32[]{:S(2)}) collective-permute-start(f32[16,8,40,4]{2,1,3,0:T(8,128)S(1)} %copy.30), channel_id=1, source_target_pairs={{1,0},{2,1},{3,2},{4,3},{5,4},{6,5},{7,6},{0,7},{9,8},{10,9},{11,1... | collective-permute-start | bytes 245768 | tf_op jit(solution)/shard_map/ppermute | solution.py:25
  46.6 9.5 %collective-permute-start.3 = (f32[16,8,40,4]{2,1,3,0:T(8,128)}, f32[16,8,40,4]{2,1,3,0:T(8,128)}, u32[]{:S(2)}, u32[]{:S(2)}) collective-permute-start(f32[16,8,40,4]{2,1,3,0:T(8,128)} %copy.32), channel_id=1, source_target_pairs={{0,1},{1,2},{2,3},{3,4},{4,5},{5,6},{6,7},{7,0},{8,9},{9,10},{10,1... | collective-permute-start | bytes 245768 | tf_op jit(solution)/shard_map/ppermute | solution.py:24
  56.1 4.7 %copy-start.11 = (f32[32,16]{0,1:T(8,128)S(1)}, f32[32,16]{0,1:T(8,128)}, u32[]{:S(2)}) copy-start(f32[32,16]{0,1:T(8,128)} %param.19) | copy-start | bytes 6148
  103.8 12.0 %copy-start.1 = (f32[16,8,32,256]{3,2,1,0:T(8,128)}, f32[16,8,32,256]{3,2,1,0:T(8,128)S(1)}, u32[]{:S(2)}) copy-start(f32[16,8,32,256]{3,2,1,0:T(8,128)S(1)} %copy.38) | copy-start | bytes 12582916
  103.8 3.6 %copy-start.7 = (f32[32,64]{1,0:T(8,128)S(1)}, f32[32,64]{1,0:T(8,128)}, u32[]{:S(2)}) copy-start(f32[32,64]{1,0:T(8,128)} %param.20) | copy-start | bytes 24580
  121.1 162.3 %reduce-scatter.5.cloned.1.call-start = ((), (), s32[]{:S(2)}) async-start(), calls=%async_computation.3 | async-start | bytes 270336 | tf_op jit(solution)/shard_map/reduce_scatter | solution.py:83
Sparse Core Ops, SparseCore 0:
  121.2 44.2 reduce-scatter.2
  170.1 113.2 reduce-scatter.4
where the time goes:
time: 295 us; the launch traced here: 290 us
  waiting for transfers between devices  162 us (55%)
  matrix products  50.3 us (17%)
  local copies, waits for them, and re-layouts  46.9 us (16%)
  between operations  14.2 us (5%)
  other arithmetic  9.5 us (3%)
  starting transfers between devices  7.01 us (2%)
    reduce_scatter x1, waiting for transfers between devices, shards(): core_part = lax.psum_scatter(reduced, 'gx', scatter_dimension=0, tiled=True)  118 us
    reduce_scatter x1, waiting for transfers between devices, shards(): lax.psum_scatter(partial_core, 'gy', scatter_dimension=1, tiled=True)  44.4 us
    dot_general x1, matrix products, shards(): jnp.einsum('rs,rzxy->szxy', stoichiometry_table, products, precision=lax....  38.4 us
    unnamed x31, local copies, waits for them, and re-layouts  13.8 us
    mul x1, other arithmetic, shards(): thermal_rate_law * chemical_share_array[first_idx]  9.48 us
    dot_general x1, matrix products, shards(): jnp.einsum('xi,szxj->ijsz', transverse_loading_horizontal, partial_y, pre...  8.32 us
    slice x2, local copies, waits for them, and re-layouts, with_halo(): last = lax.slice_in_dim(shard, length - width, length, axis=dim)  6.8 us
    gather x1, local copies, waits for them, and re-layouts, shards(): chemical_share_array[first_idx]  6.52 us
  transfers between devices with their start and end apart: 6, of which 2 were waited for; matrix products, arithmetic and copies ran while one was open for 11% of the time, Pallas kernels for 0%

commit v1 on v0

v1 whole, which is shorter than its diff:
```python
import functools
import jax
import jax.numpy as jnp
import numpy as np
import ml_dtypes
from jax import lax
from jax.experimental import pallas as pl
from jax.experimental.pallas import tpu as pltpu
from jax.sharding import PartitionSpec as P

NS, NR, NZ = 16, 32, 8
CX, CY_ = 32, 256
RANK = 64
STEP, DIFF = 0.5, 0.2
SCALE_1, SCALE_2 = 840, 5040
D1 = (672, -168, 32, -3)
D2 = (8064, -1008, 128, -9)
CENTRE = 1.0 + STEP * DIFF * 2.0 * (-205.0 / 72.0)
K_X = -STEP / SCALE_1
K_2 = STEP * DIFF / SCALE_2
F32, BF16 = jnp.float32, jnp.bfloat16
MESH = pl.DeviceIdType.MESH
HIGHEST = lax.Precision.HIGHEST
ROWS = ((8, 16), (0, 24))
X_OF = [list(range(8, 24)), list(range(0, 8)) + list(range(24, 32))]
KEPT = X_OF[1] + X_OF[0]


def tap(kind, offset):
    if offset == 0 or abs(offset) > 4:
        return 0
    if kind == 0:
        return D1[abs(offset) - 1] * (1 if offset > 0 else -1)
    return D2[abs(offset) - 1]


def stencil_tables():
    by = np.zeros((384, 512), np.float32)
    for kind in range(2):
        for out in range(256):
            for off in range(-4, 5):
                y = out + off
                row = y if 0 <= y < 256 else (256 + (y - 256) if y >= 256 else 256 + 64 + (y + 4))
                by[row, kind * 256 + out] = tap(kind, off)
    by = np.concatenate([by[:256], by[:256], by[256:], by[256:]], axis=0)
    main = np.zeros((2, 256, 256), np.float32)
    halo = np.zeros((2, 256, 128), np.float32)
    for half in range(2):
        for kind in range(2):
            for s in range(8):
                for i, x in enumerate(X_OF[half]):
                    row = kind * 128 + s * 16 + i
                    for k, xx in enumerate(KEPT):
                        main[half, row, s * 32 + k] = tap(kind, xx - x)
    for block in range(2):
        for kind in range(2):
            for s in range(8):
                for i, x in enumerate(X_OF[1]):
                    row = kind * 128 + s * 16 + i
                    for k in range(4):
                        halo[block, row, s * 8 + block * 4 + k] = tap(kind, (k - 4) - x)
                        halo[block, row, 64 + s * 8 + block * 4 + k] = tap(kind, (32 + k) - x)
    main = np.concatenate([main, main], axis=2)
    halo = np.concatenate([halo, halo], axis=2)
    bf = ml_dtypes.bfloat16
    return by.astype(bf), main.astype(bf), halo.astype(bf)


BY, AMAIN, AHALO = stencil_tables()


def split(x):
    hi = x.astype(BF16)
    return hi, (x - hi.astype(F32)).astype(BF16)


def dot(a, b, dims=((1,), (0,)), precision=None):
    return lax.dot_general(a, b, (dims, ((), ())), precision=precision, preferred_element_type=F32)


def iota(shape, dim):
    return lax.broadcasted_iota(jnp.int32, shape, dim)


def kernel(
    remote,
    ngx,
    ngy,
    act_ref,
    pref_ref,
    stoich_ref,
    load_x_ref,
    load_y_ref,
    c_hbm,
    vx_hbm,
    vy_hbm,
    t_hbm,
    by_hbm,
    am_hbm,
    ah_hbm,
    out_ref,
    core_ref,
    c,
    vx,
    vy,
    temp,
    by,
    am,
    ah,
    cs,
    xn,
    xp,
    hp,
    hn,
    yl,
    yr,
    hl,
    hr,
    w2,
    vt2,
    xb2,
    rhi,
    rlo,
    nhi,
    nlo,
    part,
    got,
    yhi,
    ylo,
    g,
    pair_got,
    gs,
    core_got,
    load_sems,
    halo_send,
    halo_recv,
    part_send,
    part_recv,
    pair_sems,
    core_send,
    core_recv,
):
    loads = []
    for k in range(NZ):
        loads.append(pltpu.make_async_copy(c_hbm.at[:, k], c.at[:, k], load_sems.at[k]))
    for k, (src, dst) in enumerate(((vx_hbm, vx), (vy_hbm, vy), (t_hbm, temp), (by_hbm, by), (am_hbm, am), (ah_hbm, ah))):
        loads.append(pltpu.make_async_copy(src, dst, load_sems.at[NZ + k]))
    for copy in loads:
        copy.start()
    if remote:
        mx, my = lax.axis_index("gx"), lax.axis_index("gy")
        par = lax.rem(mx, 2)
        chip = mx // 2
        barrier = pltpu.get_barrier_semaphore()
        gy_peer = [lax.rem(my + d, ngy) for d in range(ngy)]
        chip_peer = [lax.rem(chip + d, ngx // 2) for d in range(ngx // 2)]
        partner = mx + 1 - 2 * par
        other = lax.rem(mx + 2 * par - 1 + ngx, ngx)
        for d in range(1, ngy):
            pl.semaphore_signal(barrier, inc=1, device_id={"gx": mx, "gy": gy_peer[d]}, device_id_type=MESH)
        for d in range(1, ngx // 2):
            pl.semaphore_signal(barrier, inc=1, device_id={"gx": 2 * chip_peer[d] + par, "gy": my}, device_id_type=MESH)
        for to in (partner, other):
            pl.semaphore_signal(barrier, inc=1, device_id={"gx": to, "gy": my}, device_id_type=MESH)

    fold = dot((iota((128, 16), 0) // 8 == iota((128, 16), 1)).astype(F32), stoich_ref[...], ((1,), (1,)), HIGHEST)
    widen = (iota((32, 256), 1) // 8 == iota((32, 256), 0)).astype(F32)
    table = dot(fold, widen, precision=HIGHEST)
    scale = dot(jnp.broadcast_to(pref_ref[...], (8, 32)), widen, precision=HIGHEST)[0:1] * STEP
    table = jnp.where(iota((128, 256), 0) % 8 == iota((128, 256), 1) % 8, table * scale, 0.0)
    hi, lo = split(table)
    w2[0:128], w2[128:256] = hi, lo
    eye = (iota((64, 64), 0) == iota((64, 64), 1)).astype(F32)
    hi, lo = split(dot(eye, load_y_ref[...], ((1,), (1,)), HIGHEST))
    vt2[0:64], vt2[64:128] = hi, lo
    row = iota((512, 64), 0) // 8
    rank = 4 * (row % 32 // 2) + 2 * (row // 32) + row % 2
    pick = (rank == iota((512, 64), 1)).astype(F32)
    col = iota((32, 256), 1)
    kept = col // 128 * 16 + col % 16
    x_of = jnp.where(kept < 16, 8 + kept, jnp.where(kept < 24, kept - 16, kept))
    spread = (x_of == iota((32, 256), 0)).astype(F32)
    wide = dot(load_x_ref[...], spread, ((0,), (0,)), HIGHEST)
    wide = dot(pick, wide, precision=HIGHEST)
    wide = jnp.where(iota((512, 256), 0) % 8 == iota((512, 256), 1) % 128 // 16, wide, 0.0)
    hi, lo = split(wide)
    xb2[0:512], xb2[512:1024] = hi, lo

    for copy in loads[:NZ]:
        copy.wait()

    def pack_y(q, carry):
        lane = iota((32, 128), 1) // 4
        left = jnp.zeros((32, 128), F32)
        right = jnp.zeros((32, 128), F32)
        for p in range(32):
            s, z = q * 4 + p // 8, p % 8
            first, last = c[s, z, :, 0:128], c[s, z, :, 128:256]
            left = jnp.where(lane == p, pltpu.roll(first, 4 * p, 1) if p else first, left)
            right = jnp.where(lane == p, pltpu.roll(last, (4 * p + 4) % 128, 1) if p < 31 else last, right)
        yl[q], yr[q] = left, right
        return carry

    lax.fori_loop(0, 4, pack_y, 0)

    def pack_x(z, carry):
        low = iota((8, 256), 0) < 4
        for s in range(8):
            xn[z, s] = jnp.where(low, pltpu.roll(c[s, z, 24:32, :], 4, 0), c[s + 8, z, 24:32, :])
            xp[z, s] = jnp.where(low, c[s, z, 0:8, :], pltpu.roll(c[s + 8, z, 0:8, :], 4, 0))
        return carry

    lax.fori_loop(0, NZ, pack_x, 0)

    if remote:
        pl.semaphore_wait(barrier, ngy - 1 + ngx // 2 - 1 + 2)
        up_x, down_x = lax.rem(mx + 1, ngx), lax.rem(mx + ngx - 1, ngx)
        targets = (
            (yr, hl, mx, gy_peer[1]),
            (yl, hr, mx, gy_peer[ngy - 1]),
            (xn, hp, up_x, my),
            (xp, hn, down_x, my),
        )
        halos = [
            pltpu.make_async_remote_copy(
                src, dst, halo_send.at[k], halo_recv.at[k], device_id={"gx": tx, "gy": ty}, device_id_type=MESH
            )
            for k, (src, dst, tx, ty) in enumerate(targets)
        ]
    else:
        halos = [
            pltpu.make_async_copy(src, dst, halo_recv.at[k])
            for k, (src, dst) in enumerate(((yr, hl), (yl, hr), (xn, hp), (xp, hn)))
        ]
    for copy in halos:
        copy.start()

    def presplit(z, carry):
        for s in range(NS):
            for k, (a, b) in enumerate((ROWS[1], ROWS[0])):
                both = jnp.concatenate([c[s, z, a : a + 8, :], c[s, z, b : b + 8, :]], axis=0)
                hi, lo = split(both)
                cs[s, z, 16 * k : 16 * k + 16, 0:256] = hi
                cs[s, z, 16 * k : 16 * k + 16, 256:512] = lo
        return carry

    lax.fori_loop(0, NZ, presplit, 0)
    for copy in loads[NZ:]:
        copy.wait()

    def landed(copy):
        if remote:
            copy.wait_recv()
        else:
            copy.wait()

    landed(halos[0])
    landed(halos[1])

    def unpack_y(q, carry):
        lane = iota((32, 128), 1) < 64
        left, right = hl[q], hr[q]
        pairs = (
            jnp.where(lane, right, pltpu.roll(left, 64, 1)),
            jnp.where(lane, pltpu.roll(right, 64, 1), left),
        )
        for p in range(32):
            s, z = q * 4 + p // 8, p % 8
            k = 4 * (p % 16)
            both = pairs[p // 16]
            both = pltpu.roll(both, 128 - k, 1) if k else both
            both = jnp.concatenate([both[0:8], both[24:32], both[8:24]], axis=0)
            hi, lo = split(both)
            cs[s, z, :, 512:640] = hi
            cs[s, z, :, 640:768] = lo
        return carry

    lax.fori_loop(0, 4, unpack_y, 0)

    def step(half, z):
        kept = 0 if half == 1 else 16
        sources = []
        for t in range(2):
            r0 = ROWS[half][t]
            minus = -1.0 / temp[z, r0 : r0 + 8, :]
            for k in range(NR // 2):
                if k % 8 == 0:
                    pass
                rates = []
                for r in (2 * k, 2 * k + 1):
                    product = c[r % NS, z, r0 : r0 + 8, :] * c[(3 * r + 1) % NS, z, r0 : r0 + 8, :]
                    rates.append(jnp.exp(act_ref[r] * minus) * product)
                hi, lo = split(jnp.concatenate(rates, axis=0))
                rhi[t, 16 * k : 16 * k + 16, :] = hi
                rlo[t, 16 * k : 16 * k + 16, :] = lo
            both = dot(w2[...], rhi[t])
            sources.append(both[0:128] + both[128:256] + dot(w2[0:128], rlo[t]))
        if half == 1:
            ghost = jnp.concatenate([hp[z].reshape(64, 256), hn[z].reshape(64, 256)], axis=0)
            ghost = jnp.concatenate(split(ghost), axis=0)
        for b in range(2):
            sb = slice(8 * b, 8 * b + 8)
            oy = dot(cs[sb, z, kept : kept + 16, :].reshape(128, 768), by[...])
            field = jnp.concatenate(
                [cs[sb, z, :, 0:256].reshape(256, 256), cs[sb, z, :, 256:512].reshape(256, 256)], axis=0
            )
            ox = dot(am[half], field)
            if half == 1:
                ox = ox + dot(ah[b], ghost)
            oy = oy.reshape(8, 16, 512)
            ox1, ox2 = ox[0:128].reshape(8, 16, 256), ox[128:256].reshape(8, 16, 256)
            tiles = []
            for t in range(2):
                r0 = ROWS[half][t]
                rt = slice(8 * t, 8 * t + 8)
                fx = vx[z, r0 : r0 + 8, :] * K_X
                fy = vy[z, r0 : r0 + 8, :] * K_X
                new = c[sb, z, r0 : r0 + 8, :] * CENTRE + sources[t].reshape(16, 8, 256)[sb]
                new = new + (ox2[:, rt] + oy[:, rt, 256:512]) * K_2
                new = new + fx * ox1[:, rt] + fy * oy[:, rt, 0:256]
                out_ref[sb, z, r0 : r0 + 8, :] = new
                tiles.append(new)
            hi, lo = split(jnp.concatenate(tiles, axis=1).reshape(128, 256))
            nhi[128 * b : 128 * b + 128, :] = hi
            nlo[128 * b : 128 * b + 128, :] = lo
        both = dot(vt2[...], nhi[...], ((1,), (1,)))
        total = both[0:64] + both[64:128] + dot(vt2[0:64], nlo[...], ((1,), (1,)))
        part[:, half, z] = total.reshape(8, 8, 256)

    def send_part(half, zg, d):
        chunk = 2 * half + zg
        zs = pl.ds(4 * zg, 4)
        return pltpu.make_async_remote_copy(
            part.at[gy_peer[d], half, zs],
            got.at[d - 1, half, zs],
            part_send.at[chunk, d - 1],
            part_recv.at[chunk, d - 1],
            device_id={"gx": mx, "gy": gy_peer[d]},
            device_id_type=MESH,
        )

    for half in range(2):
        if half == 1:
            landed(halos[2])
            landed(halos[3])

        def group(zg, carry, half=half):
            def one(k, inner):
                step(half, 4 * zg + k)
                return inner

            lax.fori_loop(0, 4, one, 0)
            if remote:
                for d in range(1, ngy):
                    send_part(half, zg, d).start()
            return carry

        lax.fori_loop(0, 2, group, 0)

    if remote:
        for half in range(2):
            for zg in range(2):
                for d in range(1, ngy):
                    send_part(half, zg, d).wait_recv()
    mine = my if remote else 0
    for half in range(2):
        total = part[mine, half].reshape(64, 256)
        if remote:
            for d in range(1, ngy):
                total = total + got[d - 1, half].reshape(64, 256)
        hi, lo = split(total)
        for h in range(2):
            yhi[64 * h : 64 * h + 64, 128 * half : 128 * half + 128] = hi[:, 128 * h : 128 * h + 128]
            ylo[64 * h : 64 * h + 64, 128 * half : 128 * half + 128] = lo[:, 128 * h : 128 * h + 128]
    both = dot(xb2[...], yhi[...], ((1,), (1,)))
    total = both[0:512] + both[512:1024] + dot(xb2[0:512], ylo[...], ((1,), (1,)))
    g[...] = total.reshape(2, 16, 2, 8, 128)

    if remote:
        pair = pltpu.make_async_remote_copy(
            g.at[1 - par],
            pair_got,
            pair_sems.at[0],
            pair_sems.at[1],
            device_id={"gx": partner, "gy": my},
            device_id_type=MESH,
        )
        pair.start()
        pair.wait_recv()
        gs[...] = g[par] + pair_got[...]
        spread_out = []
        for d in range(1, ngx // 2):
            copy = pltpu.make_async_remote_copy(
                gs.at[chip_peer[d]],
                core_got.at[d - 1],
                core_send.at[d - 1],
                core_recv.at[d - 1],
                device_id={"gx": 2 * chip_peer[d] + par, "gy": my},
                device_id_type=MESH,
            )
            copy.start()
            spread_out.append(copy)
        total = gs[chip]
        for d, copy in enumerate(spread_out):
            copy.wait_recv()
            total = total + core_got[d]
    else:
        total = g[0, 0]

    a, b = iota((128, 128), 0), iota((128, 128), 1)
    swap = (a == b // 64 * 64 + b % 8 * 8 + b % 64 // 8).astype(F32)
    total = dot(total.reshape(16, 128), swap, precision=HIGHEST).reshape(2, 8, 128)
    sub, lane = iota((8, 128), 0), iota((8, 128), 1) % 64 // 8
    for i in range(2):
        tile = total[i]
        result = jnp.zeros((8, 128), F32)
        for d in range(8):
            turned = pltpu.roll(tile, d, 0) if d else tile
            if d:
                turned = jnp.where(
                    lane + d < 8, pltpu.roll(turned, 128 - 8 * d, 1), pltpu.roll(turned, 64 - 8 * d, 1)
                )
            result = jnp.where(lane == (sub - d + 8) % 8, turned, result)
        core_ref[i] = result

    if remote:
        for copy in halos:
            copy.wait_send()
        for half in range(2):
            for zg in range(2):
                for d in range(1, ngy):
                    send_part(half, zg, d).wait_send()
        pair.wait_send()
        for copy in spread_out:
            copy.wait_send()


def section(c, vx, vy, temp, pref, act, stoich, load_x, load_y, remote=True, ngx=32, ngy=8):
    vmem = pl.BlockSpec(memory_space=pltpu.VMEM)
    smem = pl.BlockSpec(memory_space=pltpu.SMEM)
    hbm = pl.BlockSpec(memory_space=pl.ANY)
    scratch = [
        pltpu.VMEM((NS, NZ, CX, CY_), F32),
        pltpu.VMEM((NZ, CX, CY_), F32),
        pltpu.VMEM((NZ, CX, CY_), F32),
        pltpu.VMEM((NZ, CX, CY_), F32),
        pltpu.VMEM(BY.shape, BF16),
        pltpu.VMEM(AMAIN.shape, BF16),
        pltpu.VMEM(AHALO.shape, BF16),
        pltpu.VMEM((NS, NZ, CX, 768), BF16),
        pltpu.VMEM((NZ, 8, 8, CY_), F32),
        pltpu.VMEM((NZ, 8, 8, CY_), F32),
        pltpu.VMEM((NZ, 8, 8, CY_), F32),
        pltpu.VMEM((NZ, 8, 8, CY_), F32),
        pltpu.VMEM((4, CX, 128), F32),
        pltpu.VMEM((4, CX, 128), F32),
        pltpu.VMEM((4, CX, 128), F32),
        pltpu.VMEM((4, CX, 128), F32),
        pltpu.VMEM((256, 256), BF16),
        pltpu.VMEM((128, 256), BF16),
        pltpu.VMEM((1024, 256), BF16),
        pltpu.VMEM((2, 256, 256), BF16),
        pltpu.VMEM((2, 256, 256), BF16),
        pltpu.VMEM((256, 256), BF16),
        pltpu.VMEM((256, 256), BF16),
        pltpu.VMEM((8, 2, NZ, 8, 256), F32),
        pltpu.VMEM((7, 2, NZ, 8, 256), F32),
        pltpu.VMEM((128, 256), BF16),
        pltpu.VMEM((128, 256), BF16),
        pltpu.VMEM((2, 16, 2, 8, 128), F32),
        pltpu.VMEM((16, 2, 8, 128), F32),
        pltpu.VMEM((16, 2, 8, 128), F32),
        pltpu.VMEM((15, 2, 8, 128), F32),
        pltpu.SemaphoreType.DMA((NZ + 6,)),
        pltpu.SemaphoreType.DMA((4,)),
        pltpu.SemaphoreType.DMA((4,)),
        pltpu.SemaphoreType.DMA((4, 7)),
        pltpu.SemaphoreType.DMA((4, 7)),
        pltpu.SemaphoreType.DMA((2,)),
        pltpu.SemaphoreType.DMA((15,)),
        pltpu.SemaphoreType.DMA((15,)),
    ]
    params = dict(vmem_limit_bytes=60 * 1024 * 1024)
    if remote:
        params.update(collective_id=0, has_side_effects=True)
    return pl.pallas_call(
        functools.partial(kernel, remote, ngx, ngy),
        name="section",
        out_shape=(
            jax.ShapeDtypeStruct((NS, NZ, CX, CY_), F32),
            jax.ShapeDtypeStruct((2, 8, 128), F32),
        ),
        in_specs=[smem, vmem, vmem, vmem, vmem] + [hbm] * 7,
        out_specs=(vmem, vmem),
        scratch_shapes=scratch,
        compiler_params=pltpu.CompilerParams(**params),
    )(
        act,
        pref.reshape(1, NR),
        stoich,
        load_x,
        load_y,
        c,
        vx,
        vy,
        temp,
        jnp.asarray(BY),
        jnp.asarray(AMAIN),
        jnp.asarray(AHALO),
    )


def solution(mesh):
    in_specs = (
        P(None, None, "gx", "gy"),
        P(None, "gx", "gy"),
        P(None, "gx", "gy"),
        P(None, "gx", "gy"),
        P(),
        P(),
        P(),
        P("gx", None),
        P("gy", None),
    )
    out_specs = (P(None, None, "gx", "gy"), P("gx", "gy", None))
    body = functools.partial(section, ngx=mesh.shape["gx"], ngy=mesh.shape["gy"])
    return jax.shard_map(body, mesh=mesh, in_specs=in_specs, out_specs=out_specs, check_vma=False)
```

time: 295 us -> 59.5 us (0.20); the launches traced: 290 us -> 59.3 us
  waiting for transfers between devices: 162 us -> 0 us
  matrix products: 50.3 us -> 0 us
  Pallas kernels: 0 us -> 50.3 us
  local copies, waits for them, and re-layouts: 46.9 us -> 8.38 us
  between operations: 14.2 us -> 0.65 us
  other arithmetic: 9.5 us -> 0 us
  starting transfers between devices: 7.01 us -> 0 us
    reduce_scatter x2 -> x0, waiting for transfers between devices: 162 us -> none  [the longest x1 118 us: shards(): core_part = lax.psum_scatter(reduced, 'gx', scatter_dimension=0, tiled=True)]
    dot_general x3 -> x0, matrix products: 50.3 us -> none  [the longest x1 38.4 us: shards(): jnp.einsum('rs,rzxy->szxy', stoichiometry_table, products, precision=lax....]
    pallas_call x0 -> x1, Pallas kernels: none -> 50.3 us  [section(): pl.pallas_call(functools.partial(kernel, remote, ngx, ngy), name='section...]
    gather x2 -> x0, local copies, waits for them, and re-layouts: 13 us -> none  [the longest x1 6.52 us: shards(): chemical_share_array[first_idx]]
    slice x4 -> x0, local copies, waits for them, and re-layouts: 10 us -> none  [the longest x2 6.8 us: with_halo(): last = lax.slice_in_dim(shard, length - width, length, axis=dim)]
    mul x1 -> x0, other arithmetic: 9.48 us -> none  [shards(): thermal_rate_law * chemical_share_array[first_idx]]
    ppermute x4 -> x0, starting transfers between devices: 6.93 us -> none  [the longest x2 3.83 us: with_halo(): after = lax.ppermute(leading, axis, down)]
    unnamed x31 -> x6, local copies, waits for them, and re-layouts: 13.8 us -> 8.38 us
  transfers between devices with their start and end apart: 6 -> 0, of which waited for: 2 -> 0; matrix products, arithmetic and copies ran while one was open for 11% -> 0% of each run, Pallas kernels for 0% -> 0%
where the time goes in v1:
time: 59.5 us; the launch traced here: 59.3 us
  Pallas kernels  50.3 us (85%)
  local copies, waits for them, and re-layouts  8.38 us (14%)
  between operations  0.65 us (1%)
    pallas_call x1, Pallas kernels, section(): pl.pallas_call(functools.partial(kernel, remote, ngx, ngy), name='section...  50.3 us
    unnamed x6, local copies, waits for them, and re-layouts  8.38 us

profile of v1, /device:TPU:1, one launch (start us, length us, event | category | flops | bytes accessed | tf_op | source)
XLA Modules:
  0.0 59.3 jit_solution(86247872570799142)
XLA Ops:
  0.6 1.4 %copy.14.stoich_ref = f32[32,16]{1,0:T(8,128)} copy(f32[32,16]{0,1:T(8,128)} %param.18) | data formatting | bytes 4096 | tf_op args[6]
  2.0 1.6 %copy.15.load_y_ref = f32[256,64]{1,0:T(8,128)} copy(f32[256,64]{0,1:T(8,128)} %param.20) | data formatting | bytes 131072 | tf_op args[8]
  3.6 50.3 %section.1 = (f32[16,8,32,256]{3,2,1,0:T(8,128)}, f32[2,8,128]{2,1,0:T(8,128)}) custom-call(f32[32]{0:T(128)} %act_ref.1, f32[1,32]{1,0:T(1,128)} %bitcast.1, f32[32,16]{1,0:T(8,128)} %copy.14.stoich_ref, f32[32,64]{1,0:T(8,128)} %load_x_ref.1, f32[256,64]{1,0:T(8,128)} %copy.15.load_y_ref, f32[16,8,32,256]{3,2,1,0:T(8,128)} %c_hbm.1, f32[8,32,256]{2,1,0:T(8,128)} %vx_hbm.1, ...), custom_call_target="tpu_custom_call" | custom-call | tf_op jit(solution)/shard_map/section/pallas_call | solution.py:486
  53.9 0.0 copy-start
  53.9 4.8 %copy.18 = f32[16,8,32,256]{3,2,1,0:T(8,128)} copy(f32[16,8,32,256]{3,2,1,0:T(8,128)} %get-tuple-element.4) | data formatting | bytes 8388608
  58.7 0.0 copy-done
  58.7 0.6 %copy.19 = f32[2,8,128]{2,1,0:T(8,128)} copy(f32[2,8,128]{2,1,0:T(8,128)S(1)} %copy-done) | data formatting | bytes 16384
Async XLA Ops:
  53.9 4.8 %copy-start = (f32[2,8,128]{2,1,0:T(8,128)S(1)}, f32[2,8,128]{2,1,0:T(8,128)}, u32[]{:S(2)}) copy-start(f32[2,8,128]{2,1,0:T(8,128)} %get-tuple-element.5) | copy-start | bytes 24580

commit v2 on v1

--- a/solution.py
+++ b/solution.py
@@ -163,15 +163,14 @@
         for to in (partner, other):
             pl.semaphore_signal(barrier, inc=1, device_id={"gx": to, "gy": my}, device_id_type=MESH)
 
-    fold = dot((iota((128, 16), 0) // 8 == iota((128, 16), 1)).astype(F32), stoich_ref[...], ((1,), (1,)), HIGHEST)
+    fold = dot((iota((128, 16), 0) // 8 == iota((128, 16), 1)).astype(F32), stoich_ref[...], precision=HIGHEST)
     widen = (iota((32, 256), 1) // 8 == iota((32, 256), 0)).astype(F32)
     table = dot(fold, widen, precision=HIGHEST)
     scale = dot(jnp.broadcast_to(pref_ref[...], (8, 32)), widen, precision=HIGHEST)[0:1] * STEP
     table = jnp.where(iota((128, 256), 0) % 8 == iota((128, 256), 1) % 8, table * scale, 0.0)
     hi, lo = split(table)
     w2[0:128], w2[128:256] = hi, lo
-    eye = (iota((64, 64), 0) == iota((64, 64), 1)).astype(F32)
-    hi, lo = split(dot(eye, load_y_ref[...], ((1,), (1,)), HIGHEST))
+    hi, lo = split(load_y_ref[...])
     vt2[0:64], vt2[64:128] = hi, lo
     row = iota((512, 64), 0) // 8
     rank = 4 * (row % 32 // 2) + 2 * (row // 32) + row % 2
@@ -438,7 +437,7 @@
 def section(c, vx, vy, temp, pref, act, stoich, load_x, load_y, remote=True, ngx=32, ngy=8):
     vmem = pl.BlockSpec(memory_space=pltpu.VMEM)
     smem = pl.BlockSpec(memory_space=pltpu.SMEM)
-    hbm = pl.BlockSpec(memory_space=pl.ANY)
+    hbm = pl.BlockSpec(memory_space=pltpu.HBM)
     scratch = [
         pltpu.VMEM((NS, NZ, CX, CY_), F32),
         pltpu.VMEM((NZ, CX, CY_), F32),
@@ -480,15 +479,15 @@
         pltpu.SemaphoreType.DMA((15,)),
         pltpu.SemaphoreType.DMA((15,)),
     ]
-    params = dict(vmem_limit_bytes=60 * 1024 * 1024)
+    params = dict(vmem_limit_bytes=59 * 1024 * 1024)
     if remote:
         params.update(collective_id=0, has_side_effects=True)
     return pl.pallas_call(
         functools.partial(kernel, remote, ngx, ngy),
         name="section",
         out_shape=(
-            jax.ShapeDtypeStruct((NS, NZ, CX, CY_), F32),
-            jax.ShapeDtypeStruct((2, 8, 128), F32),
+            pltpu.VMEM((NS, NZ, CX, CY_), F32),
+            pltpu.VMEM((2, 8, 128), F32),
         ),
         in_specs=[smem, vmem, vmem, vmem, vmem] + [hbm] * 7,
         out_specs=(vmem, vmem),
@@ -497,9 +496,9 @@
     )(
         act,
         pref.reshape(1, NR),
-        stoich,
+        stoich.T,
         load_x,
-        load_y,
+        load_y.T,
         c,
         vx,
         vy,

time: 59.5 us -> 51.8 us (0.87)
  local copies, waits for them, and re-layouts: 8.38 us -> 2.61 us
  Pallas kernels: 50.3 us -> 48.4 us
    unnamed x6 -> x2, local copies, waits for them, and re-layouts: 8.38 us -> 2.61 us
    pallas_call x1, Pallas kernels: 50.3 us -> 48.4 us  [section(): pl.pallas_call(functools.partial(kernel, remote, ngx, ngy), name='section...]
where the time goes in v2:
time: 51.8 us; the launch traced here: 51.6 us
  Pallas kernels  48.4 us (93%)
  local copies, waits for them, and re-layouts  2.61 us (5%)
  between operations  0.64 us (1%)
    pallas_call x1, Pallas kernels, section(): pl.pallas_call(functools.partial(kernel, remote, ngx, ngy), name='section...  48.4 us
    unnamed x2, local copies, waits for them, and re-layouts  2.61 us

profile of v2, /device:TPU:1, one launch (start us, length us, event | category | flops | bytes accessed | tf_op | source)
XLA Modules:
  0.0 51.6 jit_solution(8998942166931129402)
XLA Ops:
  0.6 48.4 %section.1 = (f32[16,8,32,256]{3,2,1,0:T(8,128)S(1)}, f32[2,8,128]{2,1,0:T(8,128)S(1)}) custom-call(f32[32]{0:T(128)} %act_ref.1, f32[1,32]{1,0:T(1,128)} %bitcast.5, f32[16,32]{1,0:T(8,128)} %bitcast.4, f32[32,64]{1,0:T(8,128)} %load_x_ref.1, f32[64,256]{1,0:T(8,128)} %bitcast.3, f32[16,8,32,256]{3,2,1,0:T(8,128)} %c_hbm.1, f32[8,32,256]{2,1,0:T(8,128)} %vx_hbm.1, ...), custom_call_target="tpu_custom_call" | custom-call | tf_op jit(solution)/shard_map/section/pallas_call | solution.py:485
  49.0 2.0 %copy.16 = f32[16,8,32,256]{3,2,1,0:T(8,128)} copy(f32[16,8,32,256]{3,2,1,0:T(8,128)S(1)} %get-tuple-element.2) | data formatting | bytes 8388608
  51.1 0.6 %copy.17 = f32[2,8,128]{2,1,0:T(8,128)} copy(f32[2,8,128]{2,1,0:T(8,128)S(1)} %get-tuple-element.3) | data formatting | bytes 16384

commit v3 on v2

--- a/solution.py
+++ b/solution.py
@@ -24,6 +24,8 @@
 ROWS = ((8, 16), (0, 24))
 X_OF = [list(range(8, 24)), list(range(0, 8)) + list(range(24, 32))]
 KEPT = X_OF[1] + X_OF[0]
+GY_ORDER = sorted(range(1, 8), key=lambda d: -(d // 4 + min(d % 4, 4 - d % 4)))
+GX_ORDER = sorted(range(1, 16), key=lambda d: -(2 * (d // 8) + min(d % 8, 8 - d % 8)))
 
 
 def tap(kind, offset):
@@ -152,8 +154,8 @@
         par = lax.rem(mx, 2)
         chip = mx // 2
         barrier = pltpu.get_barrier_semaphore()
-        gy_peer = [lax.rem(my + d, ngy) for d in range(ngy)]
-        chip_peer = [lax.rem(chip + d, ngx // 2) for d in range(ngx // 2)]
+        gy_peer = [lax.rem(my // 4 + f, 2) * 4 + lax.rem(my + k, 4) for f in range(2) for k in range(4)]
+        chip_peer = [lax.rem(chip // 8 + f, 2) * 8 + lax.rem(chip + k, 8) for f in range(2) for k in range(8)]
         partner = mx + 1 - 2 * par
         other = lax.rem(mx + 2 * par - 1 + ngx, ngx)
         for d in range(1, ngy):
@@ -214,25 +216,26 @@
     if remote:
         pl.semaphore_wait(barrier, ngy - 1 + ngx // 2 - 1 + 2)
         up_x, down_x = lax.rem(mx + 1, ngx), lax.rem(mx + ngx - 1, ngx)
-        targets = (
-            (yr, hl, mx, gy_peer[1]),
-            (yl, hr, mx, gy_peer[ngy - 1]),
-            (xn, hp, up_x, my),
-            (xp, hn, down_x, my),
-        )
-        halos = [
-            pltpu.make_async_remote_copy(
-                src, dst, halo_send.at[k], halo_recv.at[k], device_id={"gx": tx, "gy": ty}, device_id_type=MESH
+        def halo(k, zg=None):
+            src, dst, tx, ty = (
+                (yr, hl, mx, lax.rem(my + 1, ngy)),
+                (yl, hr, mx, lax.rem(my + ngy - 1, ngy)),
+                (xn, hp, up_x, my),
+                (xp, hn, down_x, my),
+            )[k]
+            slot = k
+            if zg is not None:
+                zs = pl.ds(2 * zg, 2)
+                src, dst, slot = src.at[zs], dst.at[zs], 2 + 4 * (k - 2) + zg
+            return pltpu.make_async_remote_copy(
+                src, dst, halo_send.at[slot], halo_recv.at[slot], device_id={"gx": tx, "gy": ty}, device_id_type=MESH
             )
-            for k, (src, dst, tx, ty) in enumerate(targets)
-        ]
-    else:
-        halos = [
-            pltpu.make_async_copy(src, dst, halo_recv.at[k])
-            for k, (src, dst) in enumerate(((yr, hl), (yl, hr), (xn, hp), (xp, hn)))
-        ]
-    for copy in halos:
-        copy.start()
+
+    for k in range(2):
+        halo(k).start()
+    for zg in range(4):
+        for k in (2, 3):
+            halo(k, zg).start()
 
     def presplit(z, carry):
         for s in range(NS):
@@ -247,14 +250,8 @@
     for copy in loads[NZ:]:
         copy.wait()
 
-    def landed(copy):
-        if remote:
-            copy.wait_recv()
-        else:
-            copy.wait()
-
-    landed(halos[0])
-    landed(halos[1])
+    halo(0).wait_recv()
+    halo(1).wait_recv()
 
     def unpack_y(q, carry):
         lane = iota((32, 128), 1) < 64
@@ -326,47 +323,38 @@
         total = both[0:64] + both[64:128] + dot(vt2[0:64], nlo[...], ((1,), (1,)))
         part[:, half, z] = total.reshape(8, 8, 256)
 
-    def send_part(half, zg, d):
-        chunk = 2 * half + zg
-        zs = pl.ds(4 * zg, 4)
+    def send_part(half, d, zs=slice(None)):
         return pltpu.make_async_remote_copy(
             part.at[gy_peer[d], half, zs],
             got.at[d - 1, half, zs],
-            part_send.at[chunk, d - 1],
-            part_recv.at[chunk, d - 1],
+            part_send.at[half, d - 1],
+            part_recv.at[half, d - 1],
             device_id={"gx": mx, "gy": gy_peer[d]},
             device_id_type=MESH,
         )
 
     for half in range(2):
-        if half == 1:
-            landed(halos[2])
-            landed(halos[3])
 
         def group(zg, carry, half=half):
             def one(k, inner):
-                step(half, 4 * zg + k)
+                step(half, 2 * zg + k)
                 return inner
 
-            lax.fori_loop(0, 4, one, 0)
-            if remote:
-                for d in range(1, ngy):
-                    send_part(half, zg, d).start()
+            if half == 1:
+                halo(2, zg).wait_recv()
+                halo(3, zg).wait_recv()
+            lax.fori_loop(0, 2, one, 0)
+            for d in GY_ORDER:
+                send_part(half, d, pl.ds(2 * zg, 2)).start()
             return carry
 
-        lax.fori_loop(0, 2, group, 0)
-
-    if remote:
-        for half in range(2):
-            for zg in range(2):
-                for d in range(1, ngy):
-                    send_part(half, zg, d).wait_recv()
-    mine = my if remote else 0
+        lax.fori_loop(0, 4, group, 0)
+
     for half in range(2):
-        total = part[mine, half].reshape(64, 256)
-        if remote:
-            for d in range(1, ngy):
-                total = total + got[d - 1, half].reshape(64, 256)
+        total = part[my, half].reshape(64, 256)
+        for d in GY_ORDER[::-1]:
+            send_part(half, d).wait_recv()
+            total = total + got[d - 1, half].reshape(64, 256)
         hi, lo = split(total)
         for h in range(2):
             yhi[64 * h : 64 * h + 64, 128 * half : 128 * half + 128] = hi[:, 128 * h : 128 * h + 128]
@@ -388,7 +376,7 @@
         pair.wait_recv()
         gs[...] = g[par] + pair_got[...]
         spread_out = []
-        for d in range(1, ngx // 2):
+        for d in GX_ORDER:
             copy = pltpu.make_async_remote_copy(
                 gs.at[chip_peer[d]],
                 core_got.at[d - 1],
@@ -400,9 +388,9 @@
             copy.start()
             spread_out.append(copy)
         total = gs[chip]
-        for d, copy in enumerate(spread_out):
+        for d, copy in list(zip(GX_ORDER, spread_out))[::-1]:
             copy.wait_recv()
-            total = total + core_got[d]
+            total = total + core_got[d - 1]
     else:
         total = g[0, 0]
 
@@ -423,12 +411,14 @@
         core_ref[i] = result
 
     if remote:
-        for copy in halos:
-            copy.wait_send()
+        for k in range(2):
+            halo(k).wait_send()
+        for zg in range(4):
+            for k in (2, 3):
+                halo(k, zg).wait_send()
         for half in range(2):
-            for zg in range(2):
-                for d in range(1, ngy):
-                    send_part(half, zg, d).wait_send()
+            for d in GY_ORDER:
+                send_part(half, d).wait_send()
         pair.wait_send()
         for copy in spread_out:
             copy.wait_send()
@@ -471,10 +461,10 @@
         pltpu.VMEM((16, 2, 8, 128), F32),
         pltpu.VMEM((15, 2, 8, 128), F32),
         pltpu.SemaphoreType.DMA((NZ + 6,)),
-        pltpu.SemaphoreType.DMA((4,)),
-        pltpu.SemaphoreType.DMA((4,)),
-        pltpu.SemaphoreType.DMA((4, 7)),
-        pltpu.SemaphoreType.DMA((4, 7)),
+        pltpu.SemaphoreType.DMA((10,)),
+        pltpu.SemaphoreType.DMA((10,)),
+        pltpu.SemaphoreType.DMA((2, 7)),
+        pltpu.SemaphoreType.DMA((2, 7)),
         pltpu.SemaphoreType.DMA((2,)),
         pltpu.SemaphoreType.DMA((15,)),
         pltpu.SemaphoreType.DMA((15,)),

time: 51.8 us -> 51.9 us (level)
  no operation moved by 1% of the time
where the time goes in v3:
time: 51.9 us; the launch traced here: 51.8 us
  Pallas kernels  48.5 us (93%)
  local copies, waits for them, and re-layouts  2.61 us (5%)
  between operations  0.64 us (1%)
    pallas_call x1, Pallas kernels, section(): pl.pallas_call(functools.partial(kernel, remote, ngx, ngy), name='section...  48.5 us
    unnamed x2, local copies, waits for them, and re-layouts  2.61 us

profile of v3, /device:TPU:1, one launch (start us, length us, event | category | flops | bytes accessed | tf_op | source)
XLA Modules:
  0.0 51.8 jit_solution(17664083281904070342)
XLA Ops:
  0.6 48.5 %section.1 = (f32[16,8,32,256]{3,2,1,0:T(8,128)S(1)}, f32[2,8,128]{2,1,0:T(8,128)S(1)}) custom-call(f32[32]{0:T(128)} %act_ref.1, f32[1,32]{1,0:T(1,128)} %bitcast.5, f32[16,32]{1,0:T(8,128)} %bitcast.4, f32[32,64]{1,0:T(8,128)} %load_x_ref.1, f32[64,256]{1,0:T(8,128)} %bitcast.3, f32[16,8,32,256]{3,2,1,0:T(8,128)} %c_hbm.1, f32[8,32,256]{2,1,0:T(8,128)} %vx_hbm.1, ...), custom_call_target="tpu_custom_call" | custom-call | tf_op jit(solution)/shard_map/section/pallas_call | solution.py:475
  49.2 2.0 %copy.16 = f32[16,8,32,256]{3,2,1,0:T(8,128)} copy(f32[16,8,32,256]{3,2,1,0:T(8,128)S(1)} %get-tuple-element.2) | data formatting | bytes 8388608
  51.2 0.6 %copy.17 = f32[2,8,128]{2,1,0:T(8,128)} copy(f32[2,8,128]{2,1,0:T(8,128)S(1)} %get-tuple-element.3) | data formatting | bytes 16384

commit v4 on v3

--- a/solution.py
+++ b/solution.py
@@ -213,6 +213,19 @@
 
     lax.fori_loop(0, NZ, pack_x, 0)
 
+    def presplit(z, carry):
+        for s in range(NS):
+            for k, (a, b) in enumerate((ROWS[1], ROWS[0])):
+                both = jnp.concatenate([c[s, z, a : a + 8, :], c[s, z, b : b + 8, :]], axis=0)
+                hi, lo = split(both)
+                cs[s, z, 16 * k : 16 * k + 16, 0:256] = hi
+                cs[s, z, 16 * k : 16 * k + 16, 256:512] = lo
+        return carry
+
+    lax.fori_loop(0, NZ, presplit, 0)
+    for copy in loads[NZ:]:
+        copy.wait()
+
     if remote:
         pl.semaphore_wait(barrier, ngy - 1 + ngx // 2 - 1 + 2)
         up_x, down_x = lax.rem(mx + 1, ngx), lax.rem(mx + ngx - 1, ngx)
@@ -236,19 +249,6 @@
     for zg in range(4):
         for k in (2, 3):
             halo(k, zg).start()
-
-    def presplit(z, carry):
-        for s in range(NS):
-            for k, (a, b) in enumerate((ROWS[1], ROWS[0])):
-                both = jnp.concatenate([c[s, z, a : a + 8, :], c[s, z, b : b + 8, :]], axis=0)
-                hi, lo = split(both)
-                cs[s, z, 16 * k : 16 * k + 16, 0:256] = hi
-                cs[s, z, 16 * k : 16 * k + 16, 256:512] = lo
-        return carry
-
-    lax.fori_loop(0, NZ, presplit, 0)
-    for copy in loads[NZ:]:
-        copy.wait()
 
     halo(0).wait_recv()
     halo(1).wait_recv()

time: 51.9 us -> 53.9 us (1.039)
  Pallas kernels: 48.5 us -> 50.5 us
    pallas_call x1, Pallas kernels: 48.5 us -> 50.5 us  [section(): pl.pallas_call(functools.partial(kernel, remote, ngx, ngy), name='section...]
where the time goes in v4:
time: 53.9 us; the launch traced here: 53.8 us
  Pallas kernels  50.5 us (94%)
  local copies, waits for them, and re-layouts  2.61 us (5%)
  between operations  0.64 us (1%)
    pallas_call x1, Pallas kernels, section(): pl.pallas_call(functools.partial(kernel, remote, ngx, ngy), name='section...  50.5 us
    unnamed x2, local copies, waits for them, and re-layouts  2.61 us

profile of v4, /device:TPU:1, one launch (start us, length us, event | category | flops | bytes accessed | tf_op | source)
XLA Modules:
  0.0 53.8 jit_solution(14202721872710884934)
XLA Ops:
  0.6 50.5 %section.1 = (f32[16,8,32,256]{3,2,1,0:T(8,128)S(1)}, f32[2,8,128]{2,1,0:T(8,128)S(1)}) custom-call(f32[32]{0:T(128)} %act_ref.1, f32[1,32]{1,0:T(1,128)} %bitcast.5, f32[16,32]{1,0:T(8,128)} %bitcast.4, f32[32,64]{1,0:T(8,128)} %load_x_ref.1, f32[64,256]{1,0:T(8,128)} %bitcast.3, f32[16,8,32,256]{3,2,1,0:T(8,128)} %c_hbm.1, f32[8,32,256]{2,1,0:T(8,128)} %vx_hbm.1, ...), custom_call_target="tpu_custom_call" | custom-call | tf_op jit(solution)/shard_map/section/pallas_call | solution.py:475
  51.2 2.0 %copy.16 = f32[16,8,32,256]{3,2,1,0:T(8,128)} copy(f32[16,8,32,256]{3,2,1,0:T(8,128)S(1)} %get-tuple-element.2) | data formatting | bytes 8388608
  53.2 0.6 %copy.17 = f32[2,8,128]{2,1,0:T(8,128)} copy(f32[2,8,128]{2,1,0:T(8,128)S(1)} %get-tuple-element.3) | data formatting | bytes 16384
